TPU v7x, 256 devices: a whole 4x4x8 slice. The times are simulated.
256 devices in a mesh: group: 8 (over z_lo, y), dev: 32 (over z_hi, x, core).
Axes of the slice: x: 4, y: 4, z: 8 (z_hi: 4, z_lo: 2; z = z_hi * 2 + z_lo), core: 2. Of those that a mesh axis runs over, the one named last changes fastest.
Arguments:
- right_side: float32 [3, 16, 64, 64, 128], P(None, 'group', 'dev'), may hold values from -60 to 60
- stiff_diag: float32 [3, 3, 16, 4096], P(None, None, 'group', 'dev'), may hold values from -0.1 to 12.75, as said below
- stiff_lower: float32 [3, 3, 13, 16, 4096], P(None, None, None, 'group', 'dev'), may hold values from -0.08 to 0.08
- fsai_diag: float32 [3, 3, 16, 4096], P(None, None, 'group', 'dev'), may hold values from -0.1 to 1, as said below
- fsai_lower: float32 [3, 3, 13, 16, 4096], P(None, None, None, 'group', 'dev'), may hold values from -0.12 to 0.12
- fsai_pattern: int32 [13, 16, 4096], P(None, 'group', 'dev'), may hold values 0 or 1
Outputs:
- solution: float32 [3, 16, 64, 64, 128], P(None, 'group', 'dev')
- residual: float32 [3, 16, 64, 64, 128], P(None, 'group', 'dev')
Inputs may be any that keep to these rules, and one draw needn't show every extreme that they name: `stiff_diag`: each 3 by 3 block is symmetric. `fsai_diag`: each 3 by 3 block is zero above its diagonal and positive on it.
All inputs are finite; a program needn't handle non-finite values. No bound on the sum of `fsai_pattern` on one device may be relied on, other than what follows from the above.
Results may differ from a plain program's by a relative error of at most 0.0003.
Values sent between devices are 32-bit elements; how exact they have to be, the bound alone decides.
A program may use at most 128 MiB of HBM per device.

v0:
```python
import jax
import jax.numpy as jnp
from jax import lax
from jax.sharding import PartitionSpec as P

ITERS = 2
highest = lax.Precision.HIGHEST
lower_offsets = [(0, 0, -1), (0, -1, -1), (0, -1, 0), (0, -1, 1)] + [
    (-1, row_step, column_step) for row_step in (-1, 0, 1) for column_step in (-1, 0, 1)
]


def with_halo(block, sides, width):
    for axis, dim in sides:
        count = lax.axis_size(axis)
        forward = [(i, i + 1) for i in range(count - 1)]
        backward = [(target, source) for source, target in forward]
        low = lax.ppermute(
            lax.slice_in_dim(block, block.shape[dim] - width, None, axis=dim), axis, forward
        )
        high = lax.ppermute(lax.slice_in_dim(block, 0, width, axis=dim), axis, backward)
        block = jnp.concatenate([low, block, high], axis=dim)
    return block


def from_behind(value, axis, steps):
    count = lax.axis_size(axis)
    first, last = (max(0, -steps), min(count, count - steps))
    return lax.ppermute(value, axis, [(source, source + steps) for source in range(first, last)])


def block_mul(coeffs, vector):
    return jnp.stack(
        [
            coeffs[target, 0][..., None] * vector[0]
            + coeffs[target, 1][..., None] * vector[1]
            + coeffs[target, 2][..., None] * vector[2]
            for target in range(3)
        ]
    )


def block_mul_transposed(coeffs, vector):
    return jnp.stack(
        [
            coeffs[0, target][..., None] * vector[0]
            + coeffs[1, target][..., None] * vector[1]
            + coeffs[2, target][..., None] * vector[2]
            for target in range(3)
        ]
    )


def pad_columns(vector):
    return jnp.pad(vector, ((0, 0), (0, 0), (0, 0), (1, 1), (0, 0)))


def local_gram(left_block, right_block):
    return jnp.einsum("azxyr,azxys->rs", left_block, right_block, precision=highest)


def combine(vector, coeffs):
    return jnp.einsum("azxyr,rs->azxys", vector, coeffs, precision=highest)


def gram_solve(matrix, right_terms):
    factor = jnp.linalg.cholesky(matrix)
    halfway = lax.linalg.triangular_solve(factor, right_terms, left_side=True, lower=True)
    return lax.linalg.triangular_solve(
        factor, halfway, left_side=True, lower=True, transpose_a=True
    )


def per_device(right_side, stiff_diag, stiff_lower, fsai_diag, fsai_lower, fsai_pattern):
    local_planes = right_side.shape[1]
    local_rows = right_side.shape[2]
    line_length = right_side.shape[3]
    slot_count = stiff_lower.shape[2]
    stiff_d = stiff_diag.reshape(3, 3, local_planes, local_rows, line_length)
    fsai_d = fsai_diag.reshape(3, 3, local_planes, local_rows, line_length)
    stiff_low = stiff_lower.reshape(3, 3, slot_count, local_planes, local_rows, line_length)
    kept = fsai_pattern.astype(jnp.float32)
    fsai_low = (fsai_lower * kept[None, None]).reshape(
        3, 3, slot_count, local_planes, local_rows, line_length
    )

    def lower_window(vector):
        rimmed = with_halo(vector, (("dev", 2),), 1)
        plane_under = from_behind(rimmed[:, local_planes - 1 :], "group", 1)
        return pad_columns(jnp.concatenate([plane_under, rimmed], axis=1))

    def gather_lower(diag_blocks, low_blocks, window_data, vector):
        result = block_mul(diag_blocks, vector)
        for slot_index, (depth_step, row_step, column_step) in enumerate(lower_offsets):
            picked = window_data[
                :,
                1 + depth_step : 1 + depth_step + local_planes,
                1 + row_step : 1 + row_step + local_rows,
                1 + column_step : 1 + column_step + line_length,
            ]
            result = result + block_mul(low_blocks[:, :, slot_index], picked)
        return result

    def push_upper(low_blocks, vector):
        buffer = None
        for slot_index, (depth_step, row_step, column_step) in enumerate(lower_offsets):
            slot_term = block_mul_transposed(low_blocks[:, :, slot_index], vector)
            placed = jnp.pad(
                slot_term,
                (
                    (0, 0),
                    (1 + depth_step, -depth_step),
                    (1 + row_step, 1 - row_step),
                    (1 + column_step, 1 - column_step),
                    (0, 0),
                ),
            )
            buffer = placed if buffer is None else buffer + placed
        inner_part = buffer[:, :, :, 1 : line_length + 1]
        rim_rows = jnp.concatenate(
            [inner_part[:, :, :1], inner_part[:, :, local_rows + 1 :]], axis=2
        )
        arrived = with_halo(rim_rows, (("dev", 2),), 1)
        core_part = inner_part[:, :, 1 : local_rows + 1]
        core_part = core_part.at[:, :, :1].add(arrived[:, :, :1])
        core_part = core_part.at[:, :, local_rows - 1 :].add(arrived[:, :, 3:])
        returned = from_behind(core_part[:, :1], "group", -1)
        return core_part[:, 1:].at[:, local_planes - 1 :].add(returned)

    def apply_fsai(vector):
        return gather_lower(fsai_d, fsai_low, lower_window(vector), vector)

    def apply_fsai_transposed(vector):
        diagonal_part = block_mul_transposed(fsai_d, vector)
        upper_sum = push_upper(fsai_low, vector)
        return diagonal_part + upper_sum

    def residual_sum(weighted):
        return lax.psum(local_gram(weighted, weighted), ("group", "dev"))

    solution = jnp.zeros_like(right_side)
    residual = right_side
    weighted = apply_fsai(residual)
    resid_gram = residual_sum(weighted)
    direction = apply_fsai_transposed(weighted)
    for iteration in range(ITERS):
        lower_sum = gather_lower(stiff_d, stiff_low, lower_window(direction), direction)
        apply_upper_sum = push_upper(stiff_low, direction)
        product = lower_sum + apply_upper_sum
        step_size = gram_solve(
            lax.psum(local_gram(direction, product), ("group", "dev")), resid_gram
        )
        solution = solution + combine(direction, step_size)
        residual = residual - combine(product, step_size)
        if iteration + 1 < ITERS:
            weighted = apply_fsai(residual)
            next_gram = residual_sum(weighted)
            precond = apply_fsai_transposed(weighted)
            conjugacy = gram_solve(resid_gram, next_gram)
            direction = precond + combine(direction, conjugacy)
            resid_gram = next_gram
    return (solution, residual)


def solution(mesh):
    return jax.shard_map(
        per_device,
        mesh=mesh,
        in_specs=(
            P(None, "group", "dev", None, None),
            P(None, None, "group", "dev"),
            P(None, None, None, "group", "dev"),
            P(None, None, "group", "dev"),
            P(None, None, None, "group", "dev"),
            P(None, "group", "dev"),
        ),
        out_specs=(P(None, "group", "dev", None, None), P(None, "group", "dev", None, None)),
        check_vma=False,
    )
```

profile of v0, /device:TPU:1, one launch (start us, length us, event | category | flops | bytes accessed | tf_op | source)
XLA Modules:
  0.0 1071.7 jit_solution(4820610917557618189)
XLA Ops:
  8.3 4.5 collective-permute-start
  12.8 1.9 collective-permute-start.1
  25.8 3.7 collective-permute-start.2
  31.3 5.2 collective-permute-done.2
  37.8 1.2 multiply_add_fusion.290
  39.0 1.2 multiply_add_fusion.289
  40.2 1.2 multiply_add_fusion.288
  41.4 1.2 multiply_add_fusion.296
  42.6 1.2 multiply_add_fusion.295
  63.6 1.4 fusion.48
  65.1 4.8 collective-permute-start.3
  71.4 1.9 collective-permute-start.4
  74.1 5.4 collective-permute-done.4
  79.6 1.3 collective-permute-start.5
  81.5 1.4 convolution_bitcast_fusion.5
  83.0 3.7 collective-permute-done.5
  87.0 3.9 collective-permute-start.6
  90.9 2.1 collective-permute-start.7
  102.7 1.4 fusion.36
  104.2 3.6 collective-permute-start.9
  107.8 1.9 collective-permute-start.10
  109.8 3.9 collective-permute-start.8
  114.2 1.6 collective-permute-done.10
  116.0 1.3 collective-permute-start.11
  117.3 4.0 collective-permute-done.8
  126.9 1.4 convolution_bitcast_fusion.6
  128.6 264.0 %all-reduce.65.cloned.1.call-done = (f32[128,128]{0,1:T(8,128)}, f32[128,128]{0,1:T(8,128)}) async-done(((f32[128,128]{0,1:T(8,128)}, f32[128,128]{0,1:T(8,128)}), (f32[128,128]{0,1:T(8,128)}, f32[128,128]{0,1:T(8,128)})) %all-reduce.65.cloned.1.call-update) | async-done | bytes 131088 | tf_op jit(solution)/shard_map/psum | solution.py:139
  394.4 11.7 %cholesky.59 = f32[128,128]{1,0:T(8,128)S(1)} custom-call(f32[128,128]{1,0:T(8,128)S(1)} %fusion.164), custom_call_target="Cholesky" | custom-call | tf_op jit(solution)/shard_map/jit(cholesky)/cholesky | solution.py:67
  407.5 9.8 custom-call.13
  420.2 4.9 collective-permute-start.12
  425.1 1.9 collective-permute-start.13
  427.0 11.7 %cholesky.70 = f32[128,128]{1,0:T(8,128)S(1)} custom-call(f32[128,128]{1,0:T(8,128)S(1)} %fusion.160), custom_call_target="Cholesky" | custom-call | tf_op jit(solution)/shard_map/jit(cholesky)/cholesky | solution.py:67
  440.4 1.8 collective-permute-start.14
  444.2 6.4 collective-permute-done.14
  450.8 1.2 multiply_add_fusion.125
  453.0 1.2 multiply_add_fusion.124
  454.2 1.2 multiply_add_fusion.123
  455.4 1.2 multiply_add_fusion.128
  457.7 1.2 multiply_add_fusion.127
  458.9 1.2 multiply_add_fusion.126
  461.2 1.2 multiply_add_fusion.131
  477.7 1.4 fusion.24
  480.0 3.3 collective-permute-start.15
  483.9 10.4 custom-call.15
  494.3 1.9 collective-permute-start.16
  496.3 1.4 convolution_bitcast_fusion.3
  498.8 3.8 collective-permute-done.16
  503.7 1.3 collective-permute-start.17
  505.0 238.5 %all-reduce.61.cloned.1.call-done = f32[128,128]{1,0:T(8,128)} async-done(((f32[128,128]{1,0:T(8,128)}), f32[128,128]{1,0:T(8,128)}) %all-reduce.61.cloned.1.call-update) | async-done | bytes 65552 | tf_op jit(solution)/shard_map/psum | solution.py:139
  756.5 2.5 collective-permute-start.18
  759.0 1.9 collective-permute-start.19
  762.6 1.4 fusion.12
  764.1 4.4 collective-permute-start.21
  768.5 1.9 collective-permute-start.22
  770.5 2.7 collective-permute-start.20
  773.6 2.9 collective-permute-done.22
  776.7 1.5 collective-permute-start.23
  778.2 1.8 collective-permute-done.20
  785.8 1.4 convolution_bitcast_fusion.1
  787.2 249.6 %all-reduce.63.cloned.1.call-done = f32[128,128]{0,1:T(8,128)} async-done(((f32[128,128]{0,1:T(8,128)}), f32[128,128]{0,1:T(8,128)}) %all-reduce.63.cloned.1.call-update) | async-done | bytes 65552 | tf_op jit(solution)/shard_map/psum | solution.py:151
  1038.6 11.7 %cholesky.81 = f32[128,128]{1,0:T(8,128)S(1)} custom-call(f32[128,128]{1,0:T(8,128)S(1)} %fusion.156), custom_call_target="Cholesky" | custom-call | tf_op jit(solution)/shard_map/jit(cholesky)/cholesky | solution.py:67
  1051.7 9.8 custom-call.17
  1062.5 1.2 convolution_subtract_fusion
  1063.7 1.2 convolution_add_fusion
  (769 shorter events, 106.5 us)
Async XLA Ops:
  7.2 385.4 %all-reduce.65.cloned.1.call-start = ((), (), s32[]{:S(2)}) async-start(), calls=%async_computation.2 | async-start | bytes 262144 | tf_op jit(solution)/shard_map/psum | solution.py:139
  8.3 17.4 %collective-permute-start = (f32[3,2,1,64,128]{4,3,2,1,0:T(8,128)S(1)}, f32[3,2,1,64,128]{4,3,2,1,0:T(8,128)S(1)}, u32[]{:S(2)}, u32[]{:S(2)}) collective-permute-start(f32[3,2,1,64,128]{4,3,2,1,0:T(8,128)S(1)} %get-tuple-element.502), channel_id=1, source_target_pairs={{0,1},{1,2},{2,3},{3,4},{4,5},{5,6},{6,7},{7,8},{8,9},{9,10},{10,1... | collective-permute-start | bytes 589832 | tf_op jit(solution)/shard_map/ppermute | solution.py:18
  12.8 13.0 %collective-permute-start.1 = (f32[3,2,1,64,128]{4,3,2,1,0:T(8,128)S(1)}, f32[3,2,1,64,128]{4,3,2,1,0:T(8,128)S(1)}, u32[]{:S(2)}, u32[]{:S(2)}) collective-permute-start(f32[3,2,1,64,128]{4,3,2,1,0:T(8,128)S(1)} %get-tuple-element.501), channel_id=1, source_target_pairs={{1,0},{2,1},{3,2},{4,3},{5,4},{6,5},{7,6},{8,7},{9,8},{10,9},{11,1... | collective-permute-start | bytes 589832 | tf_op jit(solution)/shard_map/ppermute | solution.py:21
  18.4 102.9 %copy-start.17 = (f32[2,2,64]{2,1,0:T(2,128)}, f32[2,2,64]{2,1,0:T(2,128)S(1)}, u32[]{:S(2)}) copy-start(f32[2,2,64]{2,1,0:T(2,128)S(1)} %get-tuple-element.651) | copy-start | bytes 3076
  18.4 103.0 %copy-start.19 = (f32[2,2,64]{2,1,0:T(2,128)}, f32[2,2,64]{2,1,0:T(2,128)S(1)}, u32[]{:S(2)}) copy-start(f32[2,2,64]{2,1,0:T(2,128)S(1)} %get-tuple-element.658) | copy-start | bytes 3076
  18.4 103.0 %copy-start.21 = (f32[2,2,64]{2,1,0:T(2,128)}, f32[2,2,64]{2,1,0:T(2,128)S(1)}, u32[]{:S(2)}) copy-start(f32[2,2,64]{2,1,0:T(2,128)S(1)} %get-tuple-element.659) | copy-start | bytes 3076
  18.4 103.4 %copy-start.11 = (f32[2,2,64]{2,1,0:T(2,128)}, f32[2,2,64]{2,1,0:T(2,128)S(1)}, u32[]{:S(2)}) copy-start(f32[2,2,64]{2,1,0:T(2,128)S(1)} %get-tuple-element.655) | copy-start | bytes 3076
  18.4 103.4 %copy-start.13 = (f32[2,2,64]{2,1,0:T(2,128)}, f32[2,2,64]{2,1,0:T(2,128)S(1)}, u32[]{:S(2)}) copy-start(f32[2,2,64]{2,1,0:T(2,128)S(1)} %get-tuple-element.656) | copy-start | bytes 3076
  18.5 103.4 %copy-start.15 = (f32[2,2,64]{2,1,0:T(2,128)}, f32[2,2,64]{2,1,0:T(2,128)S(1)}, u32[]{:S(2)}) copy-start(f32[2,2,64]{2,1,0:T(2,128)S(1)} %get-tuple-element.657) | copy-start | bytes 3076
  18.5 104.0 %copy-start.5 = (f32[2,2,64]{2,1,0:T(2,128)}, f32[2,2,64]{2,1,0:T(2,128)S(1)}, u32[]{:S(2)}) copy-start(f32[2,2,64]{2,1,0:T(2,128)S(1)} %get-tuple-element.652) | copy-start | bytes 3076
  18.5 104.0 %copy-start.7 = (f32[2,2,64]{2,1,0:T(2,128)}, f32[2,2,64]{2,1,0:T(2,128)S(1)}, u32[]{:S(2)}) copy-start(f32[2,2,64]{2,1,0:T(2,128)S(1)} %get-tuple-element.653) | copy-start | bytes 3076
  18.5 104.0 %copy-start.9 = (f32[2,2,64]{2,1,0:T(2,128)}, f32[2,2,64]{2,1,0:T(2,128)S(1)}, u32[]{:S(2)}) copy-start(f32[2,2,64]{2,1,0:T(2,128)S(1)} %get-tuple-element.654) | copy-start | bytes 3076
  19.2 42.9 %copy-start.130 = (f32[2,2,64]{2,1,0:T(2,128)}, f32[2,2,64]{2,1,0:T(2,128)S(1)}, u32[]{:S(2)}) copy-start(f32[2,2,64]{2,1,0:T(2,128)S(1)} %get-tuple-element.897) | copy-start | bytes 3076
  19.2 44.0 %copy-start.119 = (f32[2,2,64]{2,1,0:T(2,128)}, f32[2,2,64]{2,1,0:T(2,128)S(1)}, u32[]{:S(2)}) copy-start(f32[2,2,64]{2,1,0:T(2,128)S(1)} %get-tuple-element.896) | copy-start | bytes 3076
  19.2 44.0 %copy-start.122 = (f32[2,2,64]{2,1,0:T(2,128)}, f32[2,2,64]{2,1,0:T(2,128)S(1)}, u32[]{:S(2)}) copy-start(f32[2,2,64]{2,1,0:T(2,128)S(1)} %get-tuple-element.899) | copy-start | bytes 3076
  19.2 44.0 %copy-start.125 = (f32[2,2,64]{2,1,0:T(2,128)}, f32[2,2,64]{2,1,0:T(2,128)S(1)}, u32[]{:S(2)}) copy-start(f32[2,2,64]{2,1,0:T(2,128)S(1)} %get-tuple-element.902) | copy-start | bytes 3076
  19.8 43.4 %copy-start.134 = (f32[2,2,64]{2,1,0:T(2,128)}, f32[2,2,64]{2,1,0:T(2,128)S(1)}, u32[]{:S(2)}) copy-start(f32[2,2,64]{2,1,0:T(2,128)S(1)} %get-tuple-element.831) | copy-start | bytes 3076
  19.8 43.4 %copy-start.136 = (f32[2,2,64]{2,1,0:T(2,128)}, f32[2,2,64]{2,1,0:T(2,128)S(1)}, u32[]{:S(2)}) copy-start(f32[2,2,64]{2,1,0:T(2,128)S(1)} %get-tuple-element.833) | copy-start | bytes 3076
  19.8 43.4 %copy-start.138 = (f32[2,2,64]{2,1,0:T(2,128)}, f32[2,2,64]{2,1,0:T(2,128)S(1)}, u32[]{:S(2)}) copy-start(f32[2,2,64]{2,1,0:T(2,128)S(1)} %get-tuple-element.834) | copy-start | bytes 3076
  19.9 43.4 %copy-start.140 = (f32[2,2,64]{2,1,0:T(2,128)}, f32[2,2,64]{2,1,0:T(2,128)S(1)}, u32[]{:S(2)}) copy-start(f32[2,2,64]{2,1,0:T(2,128)S(1)} %get-tuple-element.836) | copy-start | bytes 3076
  19.9 43.4 %copy-start.142 = (f32[2,2,64]{2,1,0:T(2,128)}, f32[2,2,64]{2,1,0:T(2,128)S(1)}, u32[]{:S(2)}) copy-start(f32[2,2,64]{2,1,0:T(2,128)S(1)} %get-tuple-element.837) | copy-start | bytes 3076
  19.9 43.4 %copy-start.144 = (f32[2,2,64]{2,1,0:T(2,128)}, f32[2,2,64]{2,1,0:T(2,128)S(1)}, u32[]{:S(2)}) copy-start(f32[2,2,64]{2,1,0:T(2,128)S(1)} %get-tuple-element.839) | copy-start | bytes 3076
  23.2 101.7 %copy-start.47 = (f32[2,2,64]{2,1,0:T(2,128)}, f32[2,2,64]{2,1,0:T(2,128)S(1)}, u32[]{:S(2)}) copy-start(f32[2,2,64]{2,1,0:T(2,128)S(1)} %get-tuple-element.634) | copy-start | bytes 3076
  23.2 101.7 %copy-start.49 = (f32[2,2,64]{2,1,0:T(2,128)}, f32[2,2,64]{2,1,0:T(2,128)S(1)}, u32[]{:S(2)}) copy-start(f32[2,2,64]{2,1,0:T(2,128)S(1)} %get-tuple-element.635) | copy-start | bytes 3076
  23.2 101.7 %copy-start.51 = (f32[2,2,64]{2,1,0:T(2,128)}, f32[2,2,64]{2,1,0:T(2,128)S(1)}, u32[]{:S(2)}) copy-start(f32[2,2,64]{2,1,0:T(2,128)S(1)} %get-tuple-element.636) | copy-start | bytes 3076
  23.2 102.1 %copy-start.23 = (f32[2,2,64]{2,1,0:T(2,128)}, f32[2,2,64]{2,1,0:T(2,128)S(1)}, u32[]{:S(2)}) copy-start(f32[2,2,64]{2,1,0:T(2,128)S(1)} %get-tuple-element.633) | copy-start | bytes 3076
  23.2 102.1 %copy-start.25 = (f32[2,2,64]{2,1,0:T(2,128)}, f32[2,2,64]{2,1,0:T(2,128)S(1)}, u32[]{:S(2)}) copy-start(f32[2,2,64]{2,1,0:T(2,128)S(1)} %get-tuple-element.637) | copy-start | bytes 3076
  23.2 102.1 %copy-start.27 = (f32[2,2,64]{2,1,0:T(2,128)}, f32[2,2,64]{2,1,0:T(2,128)S(1)}, u32[]{:S(2)}) copy-start(f32[2,2,64]{2,1,0:T(2,128)S(1)} %get-tuple-element.638) | copy-start | bytes 3076
  23.2 102.1 %copy-start.29 = (f32[2,2,64]{2,1,0:T(2,128)}, f32[2,2,64]{2,1,0:T(2,128)S(1)}, u32[]{:S(2)}) copy-start(f32[2,2,64]{2,1,0:T(2,128)S(1)} %get-tuple-element.639) | copy-start | bytes 3076
  23.2 102.1 %copy-start.31 = (f32[2,2,64]{2,1,0:T(2,128)}, f32[2,2,64]{2,1,0:T(2,128)S(1)}, u32[]{:S(2)}) copy-start(f32[2,2,64]{2,1,0:T(2,128)S(1)} %get-tuple-element.640) | copy-start | bytes 3076
  23.2 102.1 %copy-start.33 = (f32[2,2,64]{2,1,0:T(2,128)}, f32[2,2,64]{2,1,0:T(2,128)S(1)}, u32[]{:S(2)}) copy-start(f32[2,2,64]{2,1,0:T(2,128)S(1)} %get-tuple-element.641) | copy-start | bytes 3076
  23.2 102.1 %copy-start.35 = (f32[2,2,64]{2,1,0:T(2,128)}, f32[2,2,64]{2,1,0:T(2,128)S(1)}, u32[]{:S(2)}) copy-start(f32[2,2,64]{2,1,0:T(2,128)S(1)} %get-tuple-element.851) | copy-start | bytes 3076
  23.2 102.1 %copy-start.37 = (f32[2,2,64]{2,1,0:T(2,128)}, f32[2,2,64]{2,1,0:T(2,128)S(1)}, u32[]{:S(2)}) copy-start(f32[2,2,64]{2,1,0:T(2,128)S(1)} %get-tuple-element.852) | copy-start | bytes 3076
  23.2 102.1 %copy-start.39 = (f32[2,2,64]{2,1,0:T(2,128)}, f32[2,2,64]{2,1,0:T(2,128)S(1)}, u32[]{:S(2)}) copy-start(f32[2,2,64]{2,1,0:T(2,128)S(1)} %get-tuple-element.853) | copy-start | bytes 3076
  23.2 102.1 %copy-start.41 = (f32[2,2,64]{2,1,0:T(2,128)}, f32[2,2,64]{2,1,0:T(2,128)S(1)}, u32[]{:S(2)}) copy-start(f32[2,2,64]{2,1,0:T(2,128)S(1)} %get-tuple-element.854) | copy-start | bytes 3076
  23.3 102.1 %copy-start.43 = (f32[2,2,64]{2,1,0:T(2,128)}, f32[2,2,64]{2,1,0:T(2,128)S(1)}, u32[]{:S(2)}) copy-start(f32[2,2,64]{2,1,0:T(2,128)S(1)} %get-tuple-element.855) | copy-start | bytes 3076
  23.3 102.1 %copy-start.45 = (f32[2,2,64]{2,1,0:T(2,128)}, f32[2,2,64]{2,1,0:T(2,128)S(1)}, u32[]{:S(2)}) copy-start(f32[2,2,64]{2,1,0:T(2,128)S(1)} %get-tuple-element.856) | copy-start | bytes 3076
  23.9 101.0 %copy-start.53 = (f32[2,2,64]{2,1,0:T(2,128)}, f32[2,2,64]{2,1,0:T(2,128)S(1)}, u32[]{:S(2)}) copy-start(f32[2,2,64]{2,1,0:T(2,128)S(1)} %get-tuple-element.615) | copy-start | bytes 3076
  25.8 10.7 collective-permute-start.2
  65.1 8.9 collective-permute-start.3
  71.4 8.0 collective-permute-start.4
  79.6 7.2 collective-permute-start.5
  87.0 14.7 %collective-permute-start.6 = (f32[3,2,1,64,128]{4,3,2,1,0:T(8,128)S(1)}, f32[3,2,1,64,128]{4,3,2,1,0:T(8,128)S(1)}, u32[]{:S(2)}, u32[]{:S(2)}) collective-permute-start(f32[3,2,1,64,128]{4,3,2,1,0:T(8,128)S(1)} %get-tuple-element.416), channel_id=1, source_target_pairs={{0,1},{1,2},{2,3},{3,4},{4,5},{5,6},{6,7},{7,8},{8,9},{9,10},{10,1... | collective-permute-start | bytes 589832 | tf_op jit(solution)/shard_map/ppermute | solution.py:18
  90.9 18.8 %collective-permute-start.7 = (f32[3,2,1,64,128]{4,3,2,1,0:T(8,128)S(1)}, f32[3,2,1,64,128]{4,3,2,1,0:T(8,128)S(1)}, u32[]{:S(2)}, u32[]{:S(2)}) collective-permute-start(f32[3,2,1,64,128]{4,3,2,1,0:T(8,128)S(1)} %get-tuple-element.417), channel_id=1, source_target_pairs={{1,0},{2,1},{3,2},{4,3},{5,4},{6,5},{7,6},{8,7},{9,8},{10,9},{11,1... | collective-permute-start | bytes 589832 | tf_op jit(solution)/shard_map/ppermute | solution.py:21
  104.2 10.0 collective-permute-start.9
  107.8 8.0 collective-permute-start.10
  109.8 11.5 %collective-permute-start.8 = (f32[3,1,4,64,128]{4,3,2,1,0:T(8,128)S(1)}, f32[3,1,4,64,128]{4,3,2,1,0:T(8,128)S(1)}, u32[]{:S(2)}, u32[]{:S(2)}) collective-permute-start(f32[3,1,4,64,128]{4,3,2,1,0:T(8,128)S(1)} %pad_maximum_fusion.5), channel_id=1, source_target_pairs={{0,32},{32,64},{64,96},{96,128},{128,160},{160,192},{192,224},{1,3... | collective-permute-start | bytes 1179656 | tf_op jit(solution)/shard_map/ppermute | solution.py:29
  116.0 10.2 collective-permute-start.11
  128.4 615.1 %all-reduce.61.cloned.1.call-start = ((), (), s32[]{:S(2)}) async-start(), calls=%async_computation | async-start | bytes 131072 | tf_op jit(solution)/shard_map/psum | solution.py:139
  420.2 20.2 %collective-permute-start.12 = (f32[3,2,1,64,128]{4,3,2,1,0:T(8,128)S(1)}, f32[3,2,1,64,128]{4,3,2,1,0:T(8,128)S(1)}, u32[]{:S(2)}, u32[]{:S(2)}) collective-permute-start(f32[3,2,1,64,128]{4,3,2,1,0:T(8,128)S(1)} %get-tuple-element.410), channel_id=1, source_target_pairs={{0,1},{1,2},{2,3},{3,4},{4,5},{5,6},{6,7},{7,8},{8,9},{9,10},{10,1... | collective-permute-start | bytes 589832 | tf_op jit(solution)/shard_map/ppermute | solution.py:18
  425.1 15.3 %collective-permute-start.13 = (f32[3,2,1,64,128]{4,3,2,1,0:T(8,128)S(1)}, f32[3,2,1,64,128]{4,3,2,1,0:T(8,128)S(1)}, u32[]{:S(2)}, u32[]{:S(2)}) collective-permute-start(f32[3,2,1,64,128]{4,3,2,1,0:T(8,128)S(1)} %get-tuple-element.411), channel_id=1, source_target_pairs={{1,0},{2,1},{3,2},{4,3},{5,4},{6,5},{7,6},{8,7},{9,8},{10,9},{11,1... | collective-permute-start | bytes 589832 | tf_op jit(solution)/shard_map/ppermute | solution.py:21
  440.4 10.2 collective-permute-start.14
  480.0 17.8 %collective-permute-start.15 = (f32[3,3,1,64,128]{4,3,2,1,0:T(8,128)}, f32[3,3,1,64,128]{4,3,2,1,0:T(8,128)}, u32[]{:S(2)}, u32[]{:S(2)}) collective-permute-start(f32[3,3,1,64,128]{4,3,2,1,0:T(8,128)} %get-tuple-element.166), channel_id=1, source_target_pairs={{0,1},{1,2},{2,3},{3,4},{4,5},{5,6},{6,7},{7,8},{8,9},{9,10},{10,1... | collective-permute-start | bytes 884744 | tf_op jit(solution)/shard_map/ppermute | solution.py:18
  494.3 8.3 collective-permute-start.16
  497.7 245.8 %copy-start.3 = (f32[1,128,128]{1,2,0:T(8,128)S(1)}, f32[1,128,128]{1,2,0:T(8,128)}, u32[]{:S(2)}) copy-start(f32[1,128,128]{1,2,0:T(8,128)} %custom-call.15) | copy-start | bytes 196612
  497.8 539.1 %all-reduce.63.cloned.1.call-start = ((), (), s32[]{:S(2)}) async-start(), calls=%async_computation.1 | async-start | bytes 131072 | tf_op jit(solution)/shard_map/psum | solution.py:151
  503.7 241.2 %collective-permute-start.17 = (f32[3,1,2,64,128]{4,3,2,1,0:T(8,128)S(1)}, f32[3,1,2,64,128]{4,3,2,1,0:T(8,128)S(1)}, u32[]{:S(2)}, u32[]{:S(2)}) collective-permute-start(f32[3,1,2,64,128]{4,3,2,1,0:T(8,128)S(1)} %slice.4621), channel_id=1, source_target_pairs={{32,0},{64,32},{96,64},{128,96},{160,128},{192,160},{224,192},{33,... | collective-permute-start | bytes 589832 | tf_op jit(solution)/shard_map/ppermute | solution.py:29
  756.5 5.1 collective-permute-start.18
  759.0 11.4 %collective-permute-start.19 = (f32[3,2,1,64,128]{4,3,2,1,0:T(8,128)S(1)}, f32[3,2,1,64,128]{4,3,2,1,0:T(8,128)S(1)}, u32[]{:S(2)}, u32[]{:S(2)}) collective-permute-start(f32[3,2,1,64,128]{4,3,2,1,0:T(8,128)S(1)} %get-tuple-element.325), channel_id=1, source_target_pairs={{1,0},{2,1},{3,2},{4,3},{5,4},{6,5},{7,6},{8,7},{9,8},{10,9},{11,1... | collective-permute-start | bytes 589832 | tf_op jit(solution)/shard_map/ppermute | solution.py:21
  764.1 9.5 collective-permute-start.21
  768.5 8.0 collective-permute-start.22
  770.5 9.5 collective-permute-start.20
  776.7 8.3 collective-permute-start.23
  785.8 275.7 %copy-start.2 = (f32[128,128]{1,0:T(8,128)S(1)}, f32[128,128]{1,0:T(8,128)}, u32[]{:S(2)}) copy-start(f32[128,128]{1,0:T(8,128)} %all-reduce.61.cloned.1.call-done) | copy-start | bytes 196612
  (243 other events, 1343.4 us)
Sparse Core Ops, SparseCore 0:
  128.5 264.0 all-reduce.64
  497.9 245.5 all-reduce.60
  787.4 249.4 all-reduce.62
where the time goes:
time: 1080 us; the launch traced here: 1070 us
  waiting for transfers between devices  788 us (73%)
  other arithmetic  168 us (16%)
  starting transfers between devices  65.3 us (6%)
  between operations  19.7 us (2%)
  local copies, waits for them, and re-layouts  17.9 us (2%)
  matrix products  12.7 us (1%)
    psum x2, waiting for transfers between devices, residual_sum(): return lax.psum(local_gram(weighted, weighted), ('group', 'dev'))  502 us
    psum x1, waiting for transfers between devices, per_device(): lax.psum(local_gram(direction, product), ('group', 'dev'))  250 us
    add x55, other arithmetic, block_mul(): coeffs[target, 0][..., None] * vector[0]  42.9 us
    add x50, other arithmetic, block_mul_transposed(): coeffs[0, target][..., None] * vector[0]  41.6 us
    another operation x9, other arithmetic, gram_solve(): factor = jnp.linalg.cholesky(matrix)  37.2 us
    ppermute x8, starting transfers between devices, with_halo(): lax.ppermute(lax.slice_in_dim(block, block.shape[dim] - width, None, axis...  32 us
    another operation x6, other arithmetic, gram_solve(): lax.linalg.triangular_solve(factor, halfway, left_side=True, lower=True,...  32 us
  transfers between devices with their start and end apart: 27, of which 13 were waited for; matrix products, arithmetic and copies ran while one was open for 7% of the time, Pallas kernels for 0%

commit v1 on v0

--- a/solution.py
+++ b/solution.py
@@ -148,7 +148,7 @@
         apply_upper_sum = push_upper(stiff_low, direction)
         product = lower_sum + apply_upper_sum
         step_size = gram_solve(
-            lax.psum(local_gram(direction, product), ("group", "dev")), resid_gram
+            lax.psum(lax.psum(local_gram(direction, product), "group"), "dev"), resid_gram
         )
         solution = solution + combine(direction, step_size)
         residual = residual - combine(product, step_size)

time: 1080 us -> 1490 us (1.38)
  waiting for transfers between devices: 788 us -> 1200 us
    psum x1 -> x4, waiting for transfers between devices: 250 us -> 679 us  [the longest x2 517 us: per_device(): lax.psum(lax.psum(local_gram(direction, product), 'group'), 'dev')]
  transfers between devices with their start and end apart: 27 -> 30, of which waited for: 13 -> 15; matrix products, arithmetic and copies ran while one was open for 7% -> 5% of each run, Pallas kernels for 0% -> 0%
where the time goes in v1:
time: 1490 us; the launch traced here: 1480 us
  waiting for transfers between devices  1200 us (81%)
  other arithmetic  167 us (11%)
  starting transfers between devices  65.3 us (4%)
  between operations  22.1 us (1%)
  local copies, waits for them, and re-layouts  18.3 us (1%)
    psum x2, waiting for transfers between devices, per_device(): lax.psum(lax.psum(local_gram(direction, product), 'group'), 'dev')  517 us
    psum x2, waiting for transfers between devices, residual_sum(): return lax.psum(local_gram(weighted, weighted), ('group', 'dev'))  493 us
    psum x2, waiting for transfers between devices, per_device(): lax.psum(local_gram(direction, product), 'group')  162 us
    add x50, other arithmetic, block_mul_transposed(): coeffs[0, target][..., None] * vector[0]  41.6 us
    add x55, other arithmetic, block_mul(): coeffs[target, 0][..., None] * vector[0]  40.3 us
    another operation x9, other arithmetic, gram_solve(): factor = jnp.linalg.cholesky(matrix)  37.2 us
    another operation x6, other arithmetic, gram_solve(): lax.linalg.triangular_solve(factor, halfway, left_side=True, lower=True,...  32 us
  transfers between devices with their start and end apart: 30, of which 15 were waited for; matrix products, arithmetic and copies ran while one was open for 5% of the time, Pallas kernels for 0%

profile of v1, /device:TPU:1, one launch (start us, length us, event | category | flops | bytes accessed | tf_op | source)
XLA Modules:
  0.0 1481.8 jit_solution(6981686148860832715)
XLA Ops:
  9.1 4.5 collective-permute-start
  13.6 1.9 collective-permute-start.1
  27.4 3.7 collective-permute-start.2
  32.9 5.2 collective-permute-done.2
  40.5 1.2 multiply_add_fusion.289
  41.7 1.2 multiply_add_fusion.288
  42.9 1.2 multiply_add_fusion.296
  44.1 1.2 multiply_add_fusion.295
  45.4 1.2 multiply_add_fusion.294
  65.3 1.4 fusion.48
  67.6 4.8 collective-permute-start.3
  72.5 1.9 collective-permute-start.4
  74.4 1.4 convolution_bitcast_fusion.5
  76.6 247.9 %all-reduce.67.cloned.1.call-done = f32[128,128]{0,1:T(8,128)} async-done(((f32[128,128]{0,1:T(8,128)}), f32[128,128]{0,1:T(8,128)}) %all-reduce.67.cloned.1.call-update) | async-done | bytes 65552 | tf_op jit(solution)/shard_map/psum | solution.py:139
  326.6 1.5 collective-permute-start.5
  328.1 11.7 cholesky.70
  340.2 2.5 collective-permute-start.6
  342.6 1.9 collective-permute-start.7
  353.8 1.4 fusion.36
  355.3 3.6 collective-permute-start.9
  359.0 1.9 collective-permute-start.10
  360.9 4.3 collective-permute-start.8
  365.6 1.4 collective-permute-done.10
  367.1 1.5 collective-permute-start.11
  368.7 4.1 collective-permute-done.8
  378.4 1.4 convolution_bitcast_fusion.6
  379.9 79.8 %all-reduce.63.cloned.1.call-done = f32[128,128]{0,1:T(8,128)} async-done(((f32[128,128]{0,1:T(8,128)}), f32[128,128]{0,1:T(8,128)}) %all-reduce.63.cloned.1.call-update) | async-done | bytes 65552 | tf_op jit(solution)/shard_map/psum | solution.py:151
  460.5 258.1 %all-reduce.65.cloned.1.call-done = f32[128,128]{0,1:T(8,128)} async-done(((f32[128,128]{0,1:T(8,128)}), f32[128,128]{0,1:T(8,128)}) %all-reduce.65.cloned.1.call-update) | async-done | bytes 65552 | tf_op jit(solution)/shard_map/psum | solution.py:151
  720.4 11.7 cholesky.59
  733.5 9.8 custom-call.13
  744.4 1.9 collective-permute-start.12
  746.3 3.8 collective-permute-start.13
  750.5 2.8 collective-permute-done.13
  753.3 3.5 collective-permute-start.14
  758.9 4.9 collective-permute-done.14
  766.2 1.2 multiply_add_fusion.124
  768.6 1.2 multiply_add_fusion.128
  771.0 1.2 multiply_add_fusion.127
  772.2 1.2 multiply_add_fusion.126
  774.5 1.2 multiply_add_fusion.131
  790.9 1.4 fusion.24
  793.3 2.1 collective-permute-start.15
  796.0 10.4 custom-call.15
  806.4 3.1 collective-permute-start.16
  809.6 1.4 convolution_bitcast_fusion.3
  812.1 2.6 collective-permute-done.16
  815.8 1.3 collective-permute-start.17
  817.1 244.7 %all-reduce.69.cloned.1.call-done = f32[128,128]{1,0:T(8,128)} async-done(((f32[128,128]{1,0:T(8,128)}), f32[128,128]{1,0:T(8,128)}) %all-reduce.69.cloned.1.call-update) | async-done | bytes 65552 | tf_op jit(solution)/shard_map/psum | solution.py:139
  1074.8 2.5 collective-permute-start.18
  1077.3 1.9 collective-permute-start.19
  1080.3 1.4 fusion.12
  1081.8 4.4 collective-permute-start.21
  1086.2 1.9 collective-permute-start.22
  1088.1 2.7 collective-permute-start.20
  1091.3 2.9 collective-permute-done.22
  1094.3 1.5 collective-permute-start.23
  1095.9 1.8 collective-permute-done.20
  1103.4 1.4 convolution_bitcast_fusion.1
  1105.2 81.7 %all-reduce.71.cloned.1.call-done = f32[128,128]{0,1:T(8,128)} async-done(((f32[128,128]{0,1:T(8,128)}), f32[128,128]{0,1:T(8,128)}) %all-reduce.71.cloned.1.call-update) | async-done | bytes 65552 | tf_op jit(solution)/shard_map/psum | solution.py:151
  1186.9 259.0 %all-reduce.73.cloned.1.call-done = f32[128,128]{0,1:T(8,128)} async-done(((f32[128,128]{0,1:T(8,128)}), f32[128,128]{0,1:T(8,128)}) %all-reduce.73.cloned.1.call-update) | async-done | bytes 65552 | tf_op jit(solution)/shard_map/psum | solution.py:151
  1447.6 11.7 cholesky.81
  1460.7 9.8 custom-call.17
  1471.5 1.2 convolution_subtract_fusion
  1472.7 1.2 convolution_add_fusion
  (808 shorter events, 107.0 us)
Async XLA Ops:
  8.0 316.4 %all-reduce.67.cloned.1.call-start = ((), (), s32[]{:S(2)}) async-start(), calls=%async_computation.2 | async-start | bytes 131072 | tf_op jit(solution)/shard_map/psum | solution.py:139
  9.1 18.1 %collective-permute-start = (f32[3,2,1,64,128]{4,3,2,1,0:T(8,128)S(1)}, f32[3,2,1,64,128]{4,3,2,1,0:T(8,128)S(1)}, u32[]{:S(2)}, u32[]{:S(2)}) collective-permute-start(f32[3,2,1,64,128]{4,3,2,1,0:T(8,128)S(1)} %get-tuple-element.500), channel_id=1, source_target_pairs={{0,1},{1,2},{2,3},{3,4},{4,5},{5,6},{6,7},{7,8},{8,9},{9,10},{10,1... | collective-permute-start | bytes 589832 | tf_op jit(solution)/shard_map/ppermute | solution.py:18
  13.6 13.7 collective-permute-start.1
  19.3 353.5 %copy-start.19 = (f32[2,2,64]{2,1,0:T(2,128)}, f32[2,2,64]{2,1,0:T(2,128)S(1)}, u32[]{:S(2)}) copy-start(f32[2,2,64]{2,1,0:T(2,128)S(1)} %get-tuple-element.649) | copy-start | bytes 3076
  19.3 353.5 %copy-start.21 = (f32[2,2,64]{2,1,0:T(2,128)}, f32[2,2,64]{2,1,0:T(2,128)S(1)}, u32[]{:S(2)}) copy-start(f32[2,2,64]{2,1,0:T(2,128)S(1)} %get-tuple-element.656) | copy-start | bytes 3076
  19.3 353.5 %copy-start.23 = (f32[2,2,64]{2,1,0:T(2,128)}, f32[2,2,64]{2,1,0:T(2,128)S(1)}, u32[]{:S(2)}) copy-start(f32[2,2,64]{2,1,0:T(2,128)S(1)} %get-tuple-element.657) | copy-start | bytes 3076
  19.3 354.0 %copy-start.13 = (f32[2,2,64]{2,1,0:T(2,128)}, f32[2,2,64]{2,1,0:T(2,128)S(1)}, u32[]{:S(2)}) copy-start(f32[2,2,64]{2,1,0:T(2,128)S(1)} %get-tuple-element.653) | copy-start | bytes 3076
  19.4 354.0 %copy-start.15 = (f32[2,2,64]{2,1,0:T(2,128)}, f32[2,2,64]{2,1,0:T(2,128)S(1)}, u32[]{:S(2)}) copy-start(f32[2,2,64]{2,1,0:T(2,128)S(1)} %get-tuple-element.654) | copy-start | bytes 3076
  19.4 354.0 %copy-start.17 = (f32[2,2,64]{2,1,0:T(2,128)}, f32[2,2,64]{2,1,0:T(2,128)S(1)}, u32[]{:S(2)}) copy-start(f32[2,2,64]{2,1,0:T(2,128)S(1)} %get-tuple-element.655) | copy-start | bytes 3076
  19.4 354.6 %copy-start.7 = (f32[2,2,64]{2,1,0:T(2,128)}, f32[2,2,64]{2,1,0:T(2,128)S(1)}, u32[]{:S(2)}) copy-start(f32[2,2,64]{2,1,0:T(2,128)S(1)} %get-tuple-element.650) | copy-start | bytes 3076
  19.4 354.6 %copy-start.9 = (f32[2,2,64]{2,1,0:T(2,128)}, f32[2,2,64]{2,1,0:T(2,128)S(1)}, u32[]{:S(2)}) copy-start(f32[2,2,64]{2,1,0:T(2,128)S(1)} %get-tuple-element.651) | copy-start | bytes 3076
  19.4 354.6 %copy-start.11 = (f32[2,2,64]{2,1,0:T(2,128)}, f32[2,2,64]{2,1,0:T(2,128)S(1)}, u32[]{:S(2)}) copy-start(f32[2,2,64]{2,1,0:T(2,128)S(1)} %get-tuple-element.652) | copy-start | bytes 3076
  20.1 43.7 %copy-start.157 = (f32[2,2,64]{2,1,0:T(2,128)}, f32[2,2,64]{2,1,0:T(2,128)S(1)}, u32[]{:S(2)}) copy-start(f32[2,2,64]{2,1,0:T(2,128)S(1)} %get-tuple-element.892) | copy-start | bytes 3076
  20.1 43.7 %copy-start.159 = (f32[2,2,64]{2,1,0:T(2,128)}, f32[2,2,64]{2,1,0:T(2,128)S(1)}, u32[]{:S(2)}) copy-start(f32[2,2,64]{2,1,0:T(2,128)S(1)} %get-tuple-element.895) | copy-start | bytes 3076
  20.1 43.7 %copy-start.161 = (f32[2,2,64]{2,1,0:T(2,128)}, f32[2,2,64]{2,1,0:T(2,128)S(1)}, u32[]{:S(2)}) copy-start(f32[2,2,64]{2,1,0:T(2,128)S(1)} %get-tuple-element.898) | copy-start | bytes 3076
  20.1 44.8 %copy-start.151 = (f32[2,2,64]{2,1,0:T(2,128)}, f32[2,2,64]{2,1,0:T(2,128)S(1)}, u32[]{:S(2)}) copy-start(f32[2,2,64]{2,1,0:T(2,128)S(1)} %get-tuple-element.894) | copy-start | bytes 3076
  20.1 44.8 %copy-start.153 = (f32[2,2,64]{2,1,0:T(2,128)}, f32[2,2,64]{2,1,0:T(2,128)S(1)}, u32[]{:S(2)}) copy-start(f32[2,2,64]{2,1,0:T(2,128)S(1)} %get-tuple-element.897) | copy-start | bytes 3076
  20.1 44.8 %copy-start.155 = (f32[2,2,64]{2,1,0:T(2,128)}, f32[2,2,64]{2,1,0:T(2,128)S(1)}, u32[]{:S(2)}) copy-start(f32[2,2,64]{2,1,0:T(2,128)S(1)} %get-tuple-element.900) | copy-start | bytes 3076
  20.8 43.0 %copy-start.187 = (f32[2,2,64]{2,1,0:T(2,128)}, f32[2,2,64]{2,1,0:T(2,128)S(1)}, u32[]{:S(2)}) copy-start(f32[2,2,64]{2,1,0:T(2,128)S(1)} %get-tuple-element.830) | copy-start | bytes 3076
  20.8 44.1 %copy-start.163 = (f32[2,2,64]{2,1,0:T(2,128)}, f32[2,2,64]{2,1,0:T(2,128)S(1)}, u32[]{:S(2)}) copy-start(f32[2,2,64]{2,1,0:T(2,128)S(1)} %get-tuple-element.829) | copy-start | bytes 3076
  20.8 44.1 %copy-start.165 = (f32[2,2,64]{2,1,0:T(2,128)}, f32[2,2,64]{2,1,0:T(2,128)S(1)}, u32[]{:S(2)}) copy-start(f32[2,2,64]{2,1,0:T(2,128)S(1)} %get-tuple-element.831) | copy-start | bytes 3076
  20.8 44.1 %copy-start.167 = (f32[2,2,64]{2,1,0:T(2,128)}, f32[2,2,64]{2,1,0:T(2,128)S(1)}, u32[]{:S(2)}) copy-start(f32[2,2,64]{2,1,0:T(2,128)S(1)} %get-tuple-element.832) | copy-start | bytes 3076
  20.8 44.1 %copy-start.169 = (f32[2,2,64]{2,1,0:T(2,128)}, f32[2,2,64]{2,1,0:T(2,128)S(1)}, u32[]{:S(2)}) copy-start(f32[2,2,64]{2,1,0:T(2,128)S(1)} %get-tuple-element.834) | copy-start | bytes 3076
  20.8 44.1 %copy-start.171 = (f32[2,2,64]{2,1,0:T(2,128)}, f32[2,2,64]{2,1,0:T(2,128)S(1)}, u32[]{:S(2)}) copy-start(f32[2,2,64]{2,1,0:T(2,128)S(1)} %get-tuple-element.835) | copy-start | bytes 3076
  20.8 44.1 %copy-start.173 = (f32[2,2,64]{2,1,0:T(2,128)}, f32[2,2,64]{2,1,0:T(2,128)S(1)}, u32[]{:S(2)}) copy-start(f32[2,2,64]{2,1,0:T(2,128)S(1)} %get-tuple-element.837) | copy-start | bytes 3076
  24.1 352.7 %copy-start.25 = (f32[2,2,64]{2,1,0:T(2,128)}, f32[2,2,64]{2,1,0:T(2,128)S(1)}, u32[]{:S(2)}) copy-start(f32[2,2,64]{2,1,0:T(2,128)S(1)} %get-tuple-element.631) | copy-start | bytes 3076
  24.1 352.7 %copy-start.27 = (f32[2,2,64]{2,1,0:T(2,128)}, f32[2,2,64]{2,1,0:T(2,128)S(1)}, u32[]{:S(2)}) copy-start(f32[2,2,64]{2,1,0:T(2,128)S(1)} %get-tuple-element.635) | copy-start | bytes 3076
  24.1 352.7 %copy-start.29 = (f32[2,2,64]{2,1,0:T(2,128)}, f32[2,2,64]{2,1,0:T(2,128)S(1)}, u32[]{:S(2)}) copy-start(f32[2,2,64]{2,1,0:T(2,128)S(1)} %get-tuple-element.636) | copy-start | bytes 3076
  24.1 352.7 %copy-start.31 = (f32[2,2,64]{2,1,0:T(2,128)}, f32[2,2,64]{2,1,0:T(2,128)S(1)}, u32[]{:S(2)}) copy-start(f32[2,2,64]{2,1,0:T(2,128)S(1)} %get-tuple-element.637) | copy-start | bytes 3076
  24.1 352.7 %copy-start.33 = (f32[2,2,64]{2,1,0:T(2,128)}, f32[2,2,64]{2,1,0:T(2,128)S(1)}, u32[]{:S(2)}) copy-start(f32[2,2,64]{2,1,0:T(2,128)S(1)} %get-tuple-element.638) | copy-start | bytes 3076
  24.1 352.7 %copy-start.35 = (f32[2,2,64]{2,1,0:T(2,128)}, f32[2,2,64]{2,1,0:T(2,128)S(1)}, u32[]{:S(2)}) copy-start(f32[2,2,64]{2,1,0:T(2,128)S(1)} %get-tuple-element.639) | copy-start | bytes 3076
  24.1 352.7 %copy-start.37 = (f32[2,2,64]{2,1,0:T(2,128)}, f32[2,2,64]{2,1,0:T(2,128)S(1)}, u32[]{:S(2)}) copy-start(f32[2,2,64]{2,1,0:T(2,128)S(1)} %get-tuple-element.849) | copy-start | bytes 3076
  24.2 352.7 %copy-start.39 = (f32[2,2,64]{2,1,0:T(2,128)}, f32[2,2,64]{2,1,0:T(2,128)S(1)}, u32[]{:S(2)}) copy-start(f32[2,2,64]{2,1,0:T(2,128)S(1)} %get-tuple-element.850) | copy-start | bytes 3076
  24.2 352.7 %copy-start.41 = (f32[2,2,64]{2,1,0:T(2,128)}, f32[2,2,64]{2,1,0:T(2,128)S(1)}, u32[]{:S(2)}) copy-start(f32[2,2,64]{2,1,0:T(2,128)S(1)} %get-tuple-element.851) | copy-start | bytes 3076
  24.2 352.7 %copy-start.43 = (f32[2,2,64]{2,1,0:T(2,128)}, f32[2,2,64]{2,1,0:T(2,128)S(1)}, u32[]{:S(2)}) copy-start(f32[2,2,64]{2,1,0:T(2,128)S(1)} %get-tuple-element.852) | copy-start | bytes 3076
  27.4 10.7 collective-permute-start.2
  67.6 257.8 %collective-permute-start.3 = (f32[3,3,1,64,128]{4,3,2,1,0:T(8,128)}, f32[3,3,1,64,128]{4,3,2,1,0:T(8,128)}, u32[]{:S(2)}, u32[]{:S(2)}) collective-permute-start(f32[3,3,1,64,128]{4,3,2,1,0:T(8,128)} %get-tuple-element.168), channel_id=1, source_target_pairs={{0,1},{1,2},{2,3},{3,4},{4,5},{5,6},{6,7},{7,8},{8,9},{9,10},{10,1... | collective-permute-start | bytes 884744 | tf_op jit(solution)/shard_map/ppermute | solution.py:18
  72.5 254.0 %collective-permute-start.4 = (f32[3,3,1,64,128]{4,3,2,1,0:T(8,128)}, f32[3,3,1,64,128]{4,3,2,1,0:T(8,128)S(1)}, u32[]{:S(2)}, u32[]{:S(2)}) collective-permute-start(f32[3,3,1,64,128]{4,3,2,1,0:T(8,128)} %get-tuple-element.167), channel_id=1, source_target_pairs={{1,0},{2,1},{3,2},{4,3},{5,4},{6,5},{7,6},{8,7},{9,8},{10,9},{11,1... | collective-permute-start | bytes 884744 | tf_op jit(solution)/shard_map/ppermute | solution.py:21
  75.8 383.9 %all-reduce.63.cloned.1.call-start = ((), (), s32[]{:S(2)}) async-start(), calls=%async_computation | async-start | bytes 131072 | tf_op jit(solution)/shard_map/psum | solution.py:151
  326.6 13.3 collective-permute-start.5
  340.2 13.3 collective-permute-start.6
  342.6 18.3 %collective-permute-start.7 = (f32[3,2,1,64,128]{4,3,2,1,0:T(8,128)S(1)}, f32[3,2,1,64,128]{4,3,2,1,0:T(8,128)S(1)}, u32[]{:S(2)}, u32[]{:S(2)}) collective-permute-start(f32[3,2,1,64,128]{4,3,2,1,0:T(8,128)S(1)} %get-tuple-element.415), channel_id=1, source_target_pairs={{1,0},{2,1},{3,2},{4,3},{5,4},{6,5},{7,6},{8,7},{9,8},{10,9},{11,1... | collective-permute-start | bytes 589832 | tf_op jit(solution)/shard_map/ppermute | solution.py:21
  355.3 10.3 collective-permute-start.9
  359.0 8.0 collective-permute-start.10
  360.9 11.8 collective-permute-start.8
  367.1 10.5 collective-permute-start.11
  379.8 338.8 %all-reduce.65.cloned.1.call-start = ((), (), s32[]{:S(2)}) async-start(), calls=%async_computation.1 | async-start | bytes 131072 | tf_op jit(solution)/shard_map/psum | solution.py:151
  459.8 602.0 %all-reduce.69.cloned.1.call-start = ((), (), s32[]{:S(2)}) async-start(), calls=%async_computation.3 | async-start | bytes 131072 | tf_op jit(solution)/shard_map/psum | solution.py:139
  744.4 6.1 collective-permute-start.12
  746.3 7.0 collective-permute-start.13
  753.3 10.5 collective-permute-start.14
  793.3 17.9 %collective-permute-start.15 = (f32[3,3,1,64,128]{4,3,2,1,0:T(8,128)}, f32[3,3,1,64,128]{4,3,2,1,0:T(8,128)}, u32[]{:S(2)}, u32[]{:S(2)}) collective-permute-start(f32[3,3,1,64,128]{4,3,2,1,0:T(8,128)} %get-tuple-element.164), channel_id=1, source_target_pairs={{0,1},{1,2},{2,3},{3,4},{4,5},{5,6},{6,7},{7,8},{8,9},{9,10},{10,1... | collective-permute-start | bytes 884744 | tf_op jit(solution)/shard_map/ppermute | solution.py:18
  806.4 8.3 collective-permute-start.16
  811.0 250.8 %copy-start.3 = (f32[1,128,128]{1,2,0:T(8,128)S(1)}, f32[1,128,128]{1,2,0:T(8,128)}, u32[]{:S(2)}) copy-start(f32[1,128,128]{1,2,0:T(8,128)} %custom-call.15) | copy-start | bytes 196612
  811.1 375.8 %all-reduce.71.cloned.1.call-start = ((), (), s32[]{:S(2)}) async-start(), calls=%async_computation.4 | async-start | bytes 131072 | tf_op jit(solution)/shard_map/psum | solution.py:151
  815.8 247.4 %collective-permute-start.17 = (f32[3,1,2,64,128]{4,3,2,1,0:T(8,128)S(1)}, f32[3,1,2,64,128]{4,3,2,1,0:T(8,128)S(1)}, u32[]{:S(2)}, u32[]{:S(2)}) collective-permute-start(f32[3,1,2,64,128]{4,3,2,1,0:T(8,128)S(1)} %slice.4621), channel_id=1, source_target_pairs={{32,0},{64,32},{96,64},{128,96},{160,128},{192,160},{224,192},{33,... | collective-permute-start | bytes 589832 | tf_op jit(solution)/shard_map/ppermute | solution.py:29
  1074.8 5.1 collective-permute-start.18
  1077.3 10.8 collective-permute-start.19
  1081.8 9.5 collective-permute-start.21
  1086.2 8.0 collective-permute-start.22
  1088.1 9.5 collective-permute-start.20
  1094.3 8.3 collective-permute-start.23
  1103.4 367.1 %copy-start.2 = (f32[128,128]{1,0:T(8,128)S(1)}, f32[128,128]{1,0:T(8,128)}, u32[]{:S(2)}) copy-start(f32[128,128]{1,0:T(8,128)} %all-reduce.69.cloned.1.call-done) | copy-start | bytes 196612
  1104.9 341.0 %all-reduce.73.cloned.1.call-start = ((), (), s32[]{:S(2)}) async-start(), calls=%async_computation.5 | async-start | bytes 131072 | tf_op jit(solution)/shard_map/psum | solution.py:151
  (261 other events, 1192.2 us)
Sparse Core Ops, SparseCore 0:
  75.9 248.4 all-reduce.66
  811.2 250.5 all-reduce.68
Sparse Core Ops, SparseCore 1:
  379.9 79.8 all-reduce.62
  462.3 256.3 all-reduce.64
  1104.9 81.8 all-reduce.70
  1189.5 256.3 all-reduce.72
